TPU v7x, 32 devices: a whole 2x2x4 slice. The times are simulated.
32 devices in a mesh: rep: 2 (over core), shard: 16 (over z, y, x).
Axes of the slice: x: 2, y: 2, z: 4, core: 2. Of those that a mesh axis runs over, the one named last changes fastest.
Arguments:
- tokens: bfloat16 [12288, 1536], P(('rep', 'shard')), may hold values from -6 to 6
- prompt_ids: int32 [32, 4], P(('rep', 'shard')), may hold values from 0 to 1
- seq_offsets: int32 [32, 4], P(('rep', 'shard')), may hold values from 32 to 64, as said below
- attn_gain: bfloat16 [1536], P('shard'), may hold values from 0.5 to 1.5
- w_query: bfloat16 [1536, 1536], P('shard'), may hold values from -0.15625 to 0.15625
- w_key: bfloat16 [1536, 1536], P('shard'), may hold values from -0.15625 to 0.15625
- w_value: bfloat16 [1536, 1536], P('shard'), may hold values from -0.15625 to 0.15625
- w_outgate: bfloat16 [1536, 1536], P('shard'), may hold values from -0.15625 to 0.15625
- w_forget: bfloat16 [1536, 24], P('shard'), may hold values from -0.15625 to 0.15625
- forget_bias: bfloat16 [24], replicated, may hold values from 1 to 8
- w_output: bfloat16 [1536, 1536], P('shard'), may hold values from -0.625 to 0.625
- ffn_gain: bfloat16 [1536], P('shard'), may hold values from 0.5 to 1.5
- w_gate: bfloat16 [1536, 4096], P('shard'), may hold values from -0.15625 to 0.15625
- w_up: bfloat16 [1536, 4096], P('shard'), may hold values from -0.15625 to 0.15625
- w_down: bfloat16 [4096, 1536], P('shard'), may hold values from -0.09375 to 0.09375
- cotangent: bfloat16 [12288, 1536], P(('rep', 'shard')), may hold values from -6 to 6
Outputs:
- layer_out: bfloat16 [12288, 1536], P(('rep', 'shard'))
- tokens_grad: float32 [12288, 1536], P(('rep', 'shard'))
- attn_gain_grad: float32 [1536], P('shard')
- query_grad: float32 [1536, 1536], P('shard')
- key_grad: float32 [1536, 1536], P('shard')
- value_grad: float32 [1536, 1536], P('shard')
- outgate_grad: float32 [1536, 1536], P('shard')
- forget_grad: float32 [1536, 24], P('shard')
- forget_bias_grad: float32 [24], replicated
- output_grad: float32 [1536, 1536], P('shard')
- ffn_gain_grad: float32 [1536], P('shard')
- gate_grad: float32 [1536, 4096], P('shard')
- up_grad: float32 [1536, 4096], P('shard')
- down_grad: float32 [4096, 1536], P('shard')
Inputs may be any that keep to these rules, and one draw needn't show every extreme that they name: `prompt_ids`: each continuation follows one of the 2 prompts of its own block. `seq_offsets`: in every block at least one continuation follows its whole prompt.
All inputs are finite; a program needn't handle non-finite values.
Results may differ from a plain program's by a relative error of at most 0.023.
Values may be sent and summed in bfloat16 or wider, within the bound.
No kernel may reach another device: no remote copies, remote signals or barrier semaphores. Data moves between devices by JAX's collectives and lax.ppermute only.
A program may use at most 320 MiB of HBM per device.

v0:
```python
import jax
import jax.numpy as jnp
from jax import lax
from jax.sharding import PartitionSpec as P

PLEN = 64
CLEN = 64
NP = 2
NC = 4
EPS = 1e-06
NEGATIVE = -1e30


def chain_mask(prompt_ids, offsets):
    positions = jnp.arange(NP * PLEN + NC * CLEN, dtype=jnp.int32)
    in_prompt = positions < NP * PLEN
    after_prompts = positions - NP * PLEN
    sequence = jnp.where(in_prompt, positions // PLEN, NP + after_prompts // CLEN)
    within = jnp.where(in_prompt, positions % PLEN, after_prompts % CLEN)
    cont_index = sequence - NP
    selector = (cont_index[:, None] == jnp.arange(NC, dtype=jnp.int32)[None, :]).astype(jnp.int32)
    owner_id = jnp.where(in_prompt, -1, jnp.sum(selector * prompt_ids[None, :], axis=1))
    reach_end = jnp.sum(selector * offsets[None, :], axis=1)
    same_seq = (sequence[:, None] == sequence[None, :]) & (within[None, :] <= within[:, None])
    from_prompt = (owner_id[:, None] == sequence[None, :]) & (within[None, :] < reach_end[:, None])
    return same_seq | from_prompt


def normalize(values):
    inverse = lax.rsqrt(jnp.mean(values * values, axis=1, keepdims=True) + EPS)
    return (values * inverse, inverse)


def norm_back(grad_scaled, scaled, inverse):
    return inverse * (grad_scaled - scaled * jnp.mean(grad_scaled * scaled, axis=1, keepdims=True))


def matmul(left_side, right_side):
    return jnp.dot(left_side, right_side, preferred_element_type=jnp.float32)


def matmul_tn(left_side, right_side):
    return lax.dot_general(
        left_side, right_side, (((0,), (0,)), ((), ())), preferred_element_type=jnp.float32
    )


def matmul_nt(left_side, right_side):
    return lax.dot_general(
        left_side, right_side, (((1,), (1,)), ((), ())), preferred_element_type=jnp.float32
    )


def decayed_scores(query_low, key_low, decay_sum, chain_ok, score_scale):
    logits = jnp.einsum("qhd,khd->hqk", query_low, key_low, preferred_element_type=jnp.float32)
    decay_t = decay_sum.T
    logits = logits * score_scale + decay_t[:, :, None] - decay_t[:, None, :]
    return jnp.where(chain_ok[None, :, :], logits, NEGATIVE)


def local(
    tokens,
    prompt_ids,
    seq_offsets,
    attn_gain,
    w_query,
    w_key,
    w_value,
    w_outgate,
    w_forget,
    forget_bias,
    w_output,
    ffn_gain,
    w_gate,
    w_up,
    w_down,
    cotangent,
):
    row_count = tokens.shape[0]
    model_width = tokens.shape[1]
    head_count = w_forget.shape[1]
    head_dim = model_width // head_count
    score_scale = head_dim ** (-0.5)
    chain_ok = chain_mask(prompt_ids[0], seq_offsets[0])
    chain_float = chain_ok.astype(jnp.float32)
    inputs = tokens.astype(jnp.float32)
    scaled1, inverse1 = normalize(inputs)
    gain_part = lax.all_gather(attn_gain, "shard", axis=0, tiled=True)
    query_part = lax.all_gather(w_query, "shard", axis=0, tiled=True)
    key_part = lax.all_gather(w_key, "shard", axis=0, tiled=True)
    value_part = lax.all_gather(w_value, "shard", axis=0, tiled=True)
    outgate_part = lax.all_gather(w_outgate, "shard", axis=0, tiled=True)
    forget_part = lax.all_gather(w_forget, "shard", axis=0, tiled=True)
    normed_part = (scaled1 * gain_part.astype(jnp.float32)).astype(jnp.bfloat16)
    gain_one = gain_part
    normed1 = normed_part
    query_proj = matmul(normed_part, query_part)
    key_proj = matmul(normed_part, key_part)
    value_proj = matmul(normed_part, value_part)
    outgate_pre = matmul(normed_part, outgate_part)
    forget_pre = matmul(normed_part, forget_part)
    query_low = query_proj.astype(jnp.bfloat16).reshape(row_count, head_count, head_dim)
    key_low = key_proj.astype(jnp.bfloat16).reshape(row_count, head_count, head_dim)
    value_low = value_proj.astype(jnp.bfloat16).reshape(row_count, head_count, head_dim)
    forget_in = forget_pre + forget_bias.astype(jnp.float32)[None, :]
    decay_sum = jnp.dot(chain_float, jax.nn.log_sigmoid(forget_in), precision=lax.Precision.HIGHEST)
    logits = decayed_scores(query_low, key_low, decay_sum, chain_ok, score_scale)
    top_score = jnp.max(logits, axis=2, keepdims=True)
    exp_scores = jnp.exp(logits - top_score)
    denominator = jnp.sum(exp_scores, axis=2, keepdims=True)
    log_total = top_score + jnp.log(denominator)
    probs_low = (exp_scores / denominator).astype(jnp.bfloat16)
    attended = jnp.einsum(
        "hqk,khd->qhd", probs_low, value_low, preferred_element_type=jnp.float32
    ).reshape(row_count, model_width)
    gate_open = jax.nn.sigmoid(outgate_pre)
    gated_low = (attended * gate_open).astype(jnp.bfloat16)
    branch_attn = matmul(gated_low, lax.all_gather(w_output, "shard", axis=0, tiled=True))
    residual = inputs + branch_attn
    scaled2, inverse2 = normalize(residual)
    gain_part = lax.all_gather(ffn_gain, "shard", axis=0, tiled=True)
    gate_part = lax.all_gather(w_gate, "shard", axis=0, tiled=True)
    up_part = lax.all_gather(w_up, "shard", axis=0, tiled=True)
    normed_part = (scaled2 * gain_part.astype(jnp.float32)).astype(jnp.bfloat16)
    gate_pre = matmul(normed_part, gate_part)
    up_pre = matmul(normed_part, up_part)
    sig_gate = jax.nn.sigmoid(gate_pre)
    silu_gate = gate_pre * sig_gate
    act_low = (silu_gate * up_pre).astype(jnp.bfloat16)
    branch_ffn = matmul(act_low, lax.all_gather(w_down, "shard", axis=0, tiled=True))
    layer_out = (residual + branch_ffn).astype(jnp.bfloat16)
    grad_out = cotangent.astype(jnp.float32)
    grad_act = matmul_nt(cotangent, lax.all_gather(w_down, "shard", axis=0, tiled=True))
    grad_gate = (grad_act * up_pre * sig_gate * (1.0 + gate_pre * (1.0 - sig_gate))).astype(
        jnp.bfloat16
    )
    grad_up = (grad_act * silu_gate).astype(jnp.bfloat16)
    gate_part = lax.all_gather(w_gate, "shard", axis=0, tiled=True)
    up_part = lax.all_gather(w_up, "shard", axis=0, tiled=True)
    contribution = matmul_nt(grad_gate, gate_part) + matmul_nt(grad_up, up_part)
    grad_normed2 = contribution
    grad_down = matmul_tn(act_low, cotangent)
    grad_gate_w = matmul_tn(normed_part, grad_gate)
    grad_up_w = matmul_tn(normed_part, grad_up)
    grad_gain2 = jnp.sum(grad_normed2 * scaled2, axis=0)
    ffn_parts = (
        lax.psum_scatter(
            grad_gain2.astype(jnp.bfloat16), "shard", scatter_dimension=0, tiled=True
        ).astype(jnp.float32),
        lax.psum_scatter(
            grad_gate_w.astype(jnp.bfloat16), "shard", scatter_dimension=0, tiled=True
        ).astype(jnp.float32),
        lax.psum_scatter(
            grad_up_w.astype(jnp.bfloat16), "shard", scatter_dimension=0, tiled=True
        ).astype(jnp.float32),
        lax.psum_scatter(
            grad_down.astype(jnp.bfloat16), "shard", scatter_dimension=0, tiled=True
        ).astype(jnp.float32),
    )
    grad_resid = grad_out + norm_back(
        grad_normed2 * gain_part.astype(jnp.float32), scaled2, inverse2
    )
    grad_attn = grad_resid.astype(jnp.bfloat16)
    grad_gated = matmul_nt(grad_attn, lax.all_gather(w_output, "shard", axis=0, tiled=True))
    grad_output_w = matmul_tn(gated_low, grad_attn)
    grad_attended = (
        (grad_gated * gate_open).astype(jnp.bfloat16).reshape(row_count, head_count, head_dim)
    )
    grad_outgate = (grad_gated * attended * gate_open * (1.0 - gate_open)).astype(jnp.bfloat16)
    logits = decayed_scores(query_low, key_low, decay_sum, chain_ok, score_scale)
    prob_full = jnp.exp(logits - log_total)
    prob_again = prob_full.astype(jnp.bfloat16)
    grad_probs = jnp.einsum(
        "qhd,khd->hqk", grad_attended, value_low, preferred_element_type=jnp.float32
    )
    grad_value = jnp.einsum(
        "hqk,qhd->khd", prob_again, grad_attended, preferred_element_type=jnp.float32
    )
    grad_logits = prob_full * (grad_probs - jnp.sum(prob_full * grad_probs, axis=2, keepdims=True))
    grad_qk = (grad_logits * score_scale).astype(jnp.bfloat16)
    grad_query = jnp.einsum("hqk,khd->qhd", grad_qk, key_low, preferred_element_type=jnp.float32)
    grad_key = jnp.einsum("hqk,qhd->khd", grad_qk, query_low, preferred_element_type=jnp.float32)
    grad_decay = (jnp.sum(grad_logits, axis=2) - jnp.sum(grad_logits, axis=1)).T
    grad_log_forget = lax.dot_general(
        chain_float, grad_decay, (((0,), (0,)), ((), ())), precision=lax.Precision.HIGHEST
    )
    grad_forget_in = grad_log_forget * jax.nn.sigmoid(-forget_in)
    grad_bias = lax.psum(jnp.sum(grad_forget_in, axis=0), ("rep", "shard"))
    grad_query_low = grad_query.reshape(row_count, model_width).astype(jnp.bfloat16)
    grad_key_low = grad_key.reshape(row_count, model_width).astype(jnp.bfloat16)
    grad_value_low = grad_value.reshape(row_count, model_width).astype(jnp.bfloat16)
    grad_forget_low = grad_forget_in.astype(jnp.bfloat16)
    query_part = lax.all_gather(w_query, "shard", axis=0, tiled=True)
    key_part = lax.all_gather(w_key, "shard", axis=0, tiled=True)
    value_part = lax.all_gather(w_value, "shard", axis=0, tiled=True)
    outgate_part = lax.all_gather(w_outgate, "shard", axis=0, tiled=True)
    forget_part = lax.all_gather(w_forget, "shard", axis=0, tiled=True)
    contribution = (
        matmul_nt(grad_query_low, query_part)
        + matmul_nt(grad_key_low, key_part)
        + matmul_nt(grad_value_low, value_part)
        + matmul_nt(grad_outgate, outgate_part)
        + matmul_nt(grad_forget_low, forget_part)
    )
    grad_query_w = matmul_tn(normed1, grad_query_low)
    grad_key_w = matmul_tn(normed1, grad_key_low)
    grad_value_w = matmul_tn(normed1, grad_value_low)
    grad_outgate_w = matmul_tn(normed1, grad_outgate)
    grad_forget_w = matmul_tn(normed1, grad_forget_low)
    grad_gain1 = jnp.sum(contribution * scaled1, axis=0)
    grad_inputs = grad_resid + norm_back(
        contribution * gain_one.astype(jnp.float32), scaled1, inverse1
    )
    attn_parts = (
        lax.psum_scatter(
            grad_gain1.astype(jnp.bfloat16), "shard", scatter_dimension=0, tiled=True
        ).astype(jnp.float32),
        lax.psum_scatter(
            grad_query_w.astype(jnp.bfloat16), "shard", scatter_dimension=0, tiled=True
        ).astype(jnp.float32),
        lax.psum_scatter(
            grad_key_w.astype(jnp.bfloat16), "shard", scatter_dimension=0, tiled=True
        ).astype(jnp.float32),
        lax.psum_scatter(
            grad_value_w.astype(jnp.bfloat16), "shard", scatter_dimension=0, tiled=True
        ).astype(jnp.float32),
        lax.psum_scatter(
            grad_outgate_w.astype(jnp.bfloat16), "shard", scatter_dimension=0, tiled=True
        ).astype(jnp.float32),
        lax.psum_scatter(
            grad_forget_w.astype(jnp.bfloat16), "shard", scatter_dimension=0, tiled=True
        ).astype(jnp.float32),
        lax.psum_scatter(
            grad_output_w.astype(jnp.bfloat16), "shard", scatter_dimension=0, tiled=True
        ).astype(jnp.float32),
    )
    summed = (
        lax.psum(attn_parts[0].astype(jnp.bfloat16), "rep").astype(jnp.float32),
        lax.psum(attn_parts[1].astype(jnp.bfloat16), "rep").astype(jnp.float32),
        lax.psum(attn_parts[2].astype(jnp.bfloat16), "rep").astype(jnp.float32),
        lax.psum(attn_parts[3].astype(jnp.bfloat16), "rep").astype(jnp.float32),
        lax.psum(attn_parts[4].astype(jnp.bfloat16), "rep").astype(jnp.float32),
        lax.psum(attn_parts[5].astype(jnp.bfloat16), "rep").astype(jnp.float32),
        lax.psum(attn_parts[6].astype(jnp.bfloat16), "rep").astype(jnp.float32),
        lax.psum(ffn_parts[0].astype(jnp.bfloat16), "rep").astype(jnp.float32),
        lax.psum(ffn_parts[1].astype(jnp.bfloat16), "rep").astype(jnp.float32),
        lax.psum(ffn_parts[2].astype(jnp.bfloat16), "rep").astype(jnp.float32),
        lax.psum(ffn_parts[3].astype(jnp.bfloat16), "rep").astype(jnp.float32),
    )
    return (
        layer_out,
        grad_inputs,
        summed[0],
        summed[1],
        summed[2],
        summed[3],
        summed[4],
        summed[5],
        grad_bias,
        summed[6],
        summed[7],
        summed[8],
        summed[9],
        summed[10],
    )


def solution(mesh):
    in_specs = (
        P(("rep", "shard"), None),
        P(("rep", "shard"), None),
        P(("rep", "shard"), None),
        P("shard"),
        P("shard", None),
        P("shard", None),
        P("shard", None),
        P("shard", None),
        P("shard", None),
        P(),
        P("shard", None),
        P("shard"),
        P("shard", None),
        P("shard", None),
        P("shard", None),
        P(("rep", "shard"), None),
    )
    out_specs = (
        P(("rep", "shard"), None),
        P(("rep", "shard"), None),
        P("shard"),
        P("shard", None),
        P("shard", None),
        P("shard", None),
        P("shard", None),
        P("shard", None),
        P(),
        P("shard", None),
        P("shard"),
        P("shard", None),
        P("shard", None),
        P("shard", None),
    )
    return jax.shard_map(local, mesh=mesh, in_specs=in_specs, out_specs=out_specs, check_vma=False)
```

profile of v0, /device:TPU:0, one launch (start us, length us, event | category | flops | bytes accessed | tf_op | source)
XLA Modules:
  0.0 2422.7 jit_solution(16868182657455146212)
XLA Ops:
  14.6 45.2 %all-reduce.5 = (bf16[1536]{0:T(1024)(128)(2,1)S(1)}, bf16[1536]{0:T(1024)(128)(2,1)S(1)}) all-reduce(bf16[1536]{0:T(1024)(128)(2,1)S(1)} %dynamic-update-slice, bf16[1536]{0:T(1024)(128)(2,1)S(1)} %dynamic-update-slice.1), channel_id=1, replica_groups=mesh['rep'=2,'shard'=16] {'shard'}, use_global_device_ids=true, to_apply=%add | all-reduce | flops 3072 | bytes 12288
  59.8 37.5 %all-gather = bf16[16,96,24]{1,2,0:T(8,128)(2,1)S(1)} all-gather(bf16[1,96,24]{1,2,0:T(8,128)(2,1)S(1)} %bitcast.93), channel_id=1, replica_groups=mesh['rep'=2,'shard'=16] {'shard'}, dimensions={0}, use_global_device_ids=true | all-gather | bytes 78336 | tf_op jit(solution)/shard_map/all_gather | solution.py:93
  105.3 71.1 %all-gather.14.cloned.1.call-done = bf16[1536,1536]{1,0:T(8,128)(2,1)} async-done(((bf16[96,1536]{1,0:T(8,128)(2,1)}), bf16[1536,1536]{1,0:T(8,128)(2,1)}) %all-gather.14.cloned.1.call-update) | async-done | bytes 4718608 | tf_op jit(solution)/shard_map/all_gather | solution.py:90
  183.5 74.1 %all-gather.10.cloned.1.call-done = bf16[1536,1536]{1,0:T(8,128)(2,1)} async-done(((bf16[96,1536]{1,0:T(8,128)(2,1)}), bf16[1536,1536]{1,0:T(8,128)(2,1)}) %all-gather.10.cloned.1.call-update) | async-done | bytes 4718608 | tf_op jit(solution)/shard_map/all_gather | solution.py:91
  280.6 9.0 fusion.10
  292.0 46.6 %all-gather.16.cloned.1.call-done = bf16[1536,1536]{1,0:T(8,128)(2,1)} async-done(((bf16[96,1536]{1,0:T(8,128)(2,1)}), bf16[1536,1536]{1,0:T(8,128)(2,1)}) %all-gather.16.cloned.1.call-update) | async-done | bytes 4718608 | tf_op jit(solution)/shard_map/all_gather | solution.py:92
  345.1 74.6 %all-gather.18.cloned.1.call-done = bf16[1536,1536]{1,0:T(8,128)(2,1)} async-done(((bf16[96,1536]{1,0:T(8,128)(2,1)}), bf16[1536,1536]{1,0:T(8,128)(2,1)}) %all-gather.18.cloned.1.call-update) | async-done | bytes 4718608 | tf_op jit(solution)/shard_map/all_gather | solution.py:118
  426.4 146.0 %all-gather.22.cloned.1.call-done = bf16[1536,4096]{1,0:T(8,128)(2,1)} async-done(((bf16[96,4096]{1,0:T(8,128)(2,1)}), bf16[1536,4096]{1,0:T(8,128)(2,1)}) %all-gather.22.cloned.1.call-update) | async-done | bytes 12582928 | tf_op jit(solution)/shard_map/all_gather | solution.py:123
  572.4 9.9 fusion.88
  582.3 142.5 %all-gather.20.cloned.1.call-done = bf16[1536,4096]{1,0:T(8,128)(2,1)} async-done(((bf16[96,4096]{1,0:T(8,128)(2,1)}), bf16[1536,4096]{1,0:T(8,128)(2,1)}) %all-gather.20.cloned.1.call-update) | async-done | bytes 12582928 | tf_op jit(solution)/shard_map/all_gather | solution.py:122
  724.8 9.9 fusion.87
  734.7 142.5 %all-gather.24.cloned.1.call-done = bf16[4096,1536]{1,0:T(8,128)(2,1)} async-done(((bf16[256,1536]{1,0:T(8,128)(2,1)}), bf16[4096,1536]{1,0:T(8,128)(2,1)}) %all-gather.24.cloned.1.call-update) | async-done | bytes 12582928 | tf_op jit(solution)/shard_map/all_gather | solution.py:130
  877.2 15.0 multiply_convert_fusion.1
  892.2 9.7 fusion.89
  902.0 9.3 multiply_reduce_fusion.1
  948.4 22.3 fusion.83
  970.7 8.2 fusion.30
  997.1 11.3 convolution_convert_fusion
  1008.5 11.3 convolution_convert_fusion.1
  1020.0 11.4 convolution_convert_fusion.2
  1048.1 38.9 %psum.90 = f32[24]{0:T(128)} all-reduce(f32[24]{0:T(128)S(1)} %get-tuple-element.53), channel_id=1, replica_groups=mesh['rep'=2,'shard'=16] {'rep','shard'}, use_global_device_ids=true, to_apply=%region_25.26 | all-reduce | flops 24 | bytes 192 | tf_op jit(solution)/shard_map/psum | solution.py:188
  1086.9 110.5 %reduce-scatter.18.cloned.1.call-done = bf16[96,1536]{1,0:T(8,128)(2,1)} async-done(((bf16[1536,1536]{1,0:T(8,128)(2,1)}), bf16[96,1536]{1,0:T(8,128)(2,1)}) %reduce-scatter.18.cloned.1.call-update) | async-done | bytes 294928 | tf_op jit(solution)/shard_map/reduce_scatter | solution.py:227
  1197.4 143.3 %reduce-scatter.16.cloned.1.call-done = bf16[96,1536]{1,0:T(8,128)(2,1)} async-done(((bf16[1536,1536]{1,0:T(8,128)(2,1)}), bf16[96,1536]{1,0:T(8,128)(2,1)}) %reduce-scatter.16.cloned.1.call-update) | async-done | bytes 294928 | tf_op jit(solution)/shard_map/reduce_scatter | solution.py:224
  1340.7 142.9 %reduce-scatter.14.cloned.1.call-done = bf16[96,1536]{1,0:T(8,128)(2,1)} async-done(((bf16[1536,1536]{1,0:T(8,128)(2,1)}), bf16[96,1536]{1,0:T(8,128)(2,1)}) %reduce-scatter.14.cloned.1.call-update) | async-done | bytes 294928 | tf_op jit(solution)/shard_map/reduce_scatter | solution.py:221
  1483.7 143.1 %reduce-scatter.12.cloned.1.call-done = bf16[96,1536]{1,0:T(8,128)(2,1)} async-done(((bf16[1536,1536]{1,0:T(8,128)(2,1)}), bf16[96,1536]{1,0:T(8,128)(2,1)}) %reduce-scatter.12.cloned.1.call-update) | async-done | bytes 294928 | tf_op jit(solution)/shard_map/reduce_scatter | solution.py:218
  1626.7 207.2 %reduce-scatter.26.cloned.1.call-done = bf16[256,1536]{1,0:T(8,128)(2,1)} async-done(((bf16[4096,1536]{1,0:T(8,128)(2,1)}), bf16[256,1536]{1,0:T(8,128)(2,1)}) %reduce-scatter.26.cloned.1.call-update) | async-done | bytes 786448 | tf_op jit(solution)/shard_map/reduce_scatter | solution.py:156
  1834.0 207.7 %reduce-scatter.24.cloned.1.call-done = bf16[96,4096]{1,0:T(8,128)(2,1)} async-done(((bf16[1536,4096]{1,0:T(8,128)(2,1)}), bf16[96,4096]{1,0:T(8,128)(2,1)}) %reduce-scatter.24.cloned.1.call-update) | async-done | bytes 786448 | tf_op jit(solution)/shard_map/reduce_scatter | solution.py:153
  2041.7 207.7 %reduce-scatter.22.cloned.1.call-done = bf16[96,4096]{1,0:T(8,128)(2,1)} async-done(((bf16[1536,4096]{1,0:T(8,128)(2,1)}), bf16[96,4096]{1,0:T(8,128)(2,1)}) %reduce-scatter.22.cloned.1.call-update) | async-done | bytes 786448 | tf_op jit(solution)/shard_map/reduce_scatter | solution.py:150
  2262.4 41.8 %all-reduce.4 = (bf16[1536]{0:T(1024)(128)(2,1)}, bf16[1536]{0:T(1024)(128)(2,1)}) all-reduce(bf16[1536]{0:T(1024)(128)(2,1)S(1)} %get-tuple-element.18, bf16[1536]{0:T(1024)(128)(2,1)} %get-tuple-element.16), channel_id=2, replica_groups=mesh['rep'=2,'shard'=16] {'shard'}, use_global_device_ids=true, to_apply=%region_12.13.clone | all-reduce | flops 3072 | bytes 12288
  2310.8 9.3 fusion.19
  2320.1 56.9 %reduce-scatter.28.cloned.1.call-done = bf16[96,24]{1,0:T(8,128)(2,1)} async-done(((bf16[1536,24]{1,0:T(8,128)(2,1)}), bf16[96,24]{1,0:T(8,128)(2,1)}) %reduce-scatter.28.cloned.1.call-update) | async-done | bytes 4624
  2382.0 22.1 all-reduce.10.cloned.1.call-done
  (191 shorter events, 166.9 us)
Async XLA Ops:
  7.2 52.6 %copy-start.30 = (bf16[96,24]{0,1:T(8,128)(2,1)S(1)}, bf16[96,24]{0,1:T(8,128)(2,1)}, u32[]{:S(2)}) copy-start(bf16[96,24]{0,1:T(8,128)(2,1)} %param.24) | copy-start | bytes 13828
  7.2 90.3 %copy-start.33 = (s32[1,4]{1,0:T(1,128)S(1)}, s32[1,4]{1,0:T(1,128)}, u32[]{:S(2)}) copy-start(s32[1,4]{1,0:T(1,128)} %param.18) | copy-start | bytes 52
  7.2 90.3 %copy-start.32 = (s32[1,4]{1,0:T(1,128)S(1)}, s32[1,4]{1,0:T(1,128)}, u32[]{:S(2)}) copy-start(s32[1,4]{1,0:T(1,128)} %param.17) | copy-start | bytes 52
  7.3 90.4 %copy-start = (bf16[384,1536]{1,0:T(8,128)(2,1)S(1)}, bf16[384,1536]{1,0:T(8,128)(2,1)}, u32[]{:S(2)}) copy-start(bf16[384,1536]{1,0:T(8,128)(2,1)} %param.16) | copy-start | bytes 3538948
  7.3 92.6 %all-gather.12.cloned.1.call-start = ((), (), s32[]{:S(2)}) async-start(), calls=%async_computation.10 | async-start | bytes 5013504 | tf_op jit(solution)/shard_map/all_gather | solution.py:89
  8.0 168.4 %all-gather.14.cloned.1.call-start = ((), (), s32[]{:S(2)}) async-start(), calls=%async_computation.11 | async-start | bytes 5013504 | tf_op jit(solution)/shard_map/all_gather | solution.py:90
  8.7 248.8 %all-gather.10.cloned.1.call-start = ((), (), s32[]{:S(2)}) async-start(), calls=%async_computation.9 | async-start | bytes 5013504 | tf_op jit(solution)/shard_map/all_gather | solution.py:91
  9.5 329.1 %all-gather.16.cloned.1.call-start = ((), (), s32[]{:S(2)}) async-start(), calls=%async_computation.12 | async-start | bytes 5013504 | tf_op jit(solution)/shard_map/all_gather | solution.py:92
  10.1 409.6 %all-gather.18.cloned.1.call-start = ((), (), s32[]{:S(2)}) async-start(), calls=%async_computation.13 | async-start | bytes 5013504 | tf_op jit(solution)/shard_map/all_gather | solution.py:118
  10.6 561.7 %all-gather.22.cloned.1.call-start = ((), (), s32[]{:S(2)}) async-start(), calls=%async_computation.15 | async-start | bytes 13369344 | tf_op jit(solution)/shard_map/all_gather | solution.py:123
  11.2 713.6 %all-gather.20.cloned.1.call-start = ((), (), s32[]{:S(2)}) async-start(), calls=%async_computation.14 | async-start | bytes 13369344 | tf_op jit(solution)/shard_map/all_gather | solution.py:122
  12.0 865.2 %all-gather.24.cloned.1.call-start = ((), (), s32[]{:S(2)}) async-start(), calls=%async_computation.16 | async-start | bytes 13369344 | tf_op jit(solution)/shard_map/all_gather | solution.py:130
  12.7 1074.2 %reduce-scatter.20.cloned.1.call-start = ((), (), s32[]{:S(2)}) async-start(), calls=%async_computation.21 | async-start | bytes 5013504 | tf_op jit(solution)/shard_map/reduce_scatter | solution.py:233
  105.2 160.1 %copy-start.5 = (bf16[384,1536]{0,1:T(8,128)(2,1)}, bf16[384,1536]{0,1:T(8,128)(2,1)S(1)}, u32[]{:S(2)}) copy-start(bf16[384,1536]{0,1:T(8,128)(2,1)S(1)} %copy.67) | copy-start | bytes 3538948
  183.5 81.9 %copy-start.4 = (bf16[384,1536]{0,1:T(8,128)(2,1)}, bf16[384,1536]{0,1:T(8,128)(2,1)S(1)}, u32[]{:S(2)}) copy-start(bf16[384,1536]{0,1:T(8,128)(2,1)S(1)} %copy.68) | copy-start | bytes 3538948
  280.6 9.1 copy-start.22
  292.0 53.1 %copy-start.1 = (f32[384,1536]{1,0:T(8,128)}, f32[384,1536]{1,0:T(8,128)S(1)}, u32[]{:S(2)}) copy-start(f32[384,1536]{1,0:T(8,128)S(1)} %copy.71) | copy-start | bytes 7077892
  424.4 477.5 %copy-start.2 = (f32[384,1536]{1,0:T(8,128)}, f32[384,1536]{1,0:T(8,128)S(1)}, u32[]{:S(2)}) copy-start(f32[384,1536]{1,0:T(8,128)S(1)} %get-tuple-element.49) | copy-start | bytes 7077892
  892.2 9.8 copy-start.29
  892.2 9.8 copy-start.40
  902.0 9.3 copy-start.6
  918.1 279.3 %reduce-scatter.18.cloned.1.call-start = ((), (), s32[]{:S(2)}) async-start(), calls=%async_computation.20 | async-start | bytes 5013504 | tf_op jit(solution)/shard_map/reduce_scatter | solution.py:227
  918.2 7.9 copy-start.27
  930.6 410.2 %reduce-scatter.16.cloned.1.call-start = ((), (), s32[]{:S(2)}) async-start(), calls=%async_computation.19 | async-start | bytes 5013504 | tf_op jit(solution)/shard_map/reduce_scatter | solution.py:224
  948.4 535.3 %reduce-scatter.14.cloned.1.call-start = ((), (), s32[]{:S(2)}) async-start(), calls=%async_computation.18 | async-start | bytes 5013504 | tf_op jit(solution)/shard_map/reduce_scatter | solution.py:221
  984.5 642.2 %reduce-scatter.12.cloned.1.call-start = ((), (), s32[]{:S(2)}) async-start(), calls=%async_computation.17 | async-start | bytes 5013504 | tf_op jit(solution)/shard_map/reduce_scatter | solution.py:218
  997.1 836.9 %reduce-scatter.26.cloned.1.call-start = ((), (), s32[]{:S(2)}) async-start(), calls=%async_computation.24 | async-start | bytes 13369344 | tf_op jit(solution)/shard_map/reduce_scatter | solution.py:156
  1008.5 1033.2 %reduce-scatter.24.cloned.1.call-start = ((), (), s32[]{:S(2)}) async-start(), calls=%async_computation.23 | async-start | bytes 13369344 | tf_op jit(solution)/shard_map/reduce_scatter | solution.py:153
  1019.9 1229.5 %reduce-scatter.22.cloned.1.call-start = ((), (), s32[]{:S(2)}) async-start(), calls=%async_computation.22 | async-start | bytes 13369344 | tf_op jit(solution)/shard_map/reduce_scatter | solution.py:150
  1031.4 1345.7 %reduce-scatter.28.cloned.1.call-start = ((), (), s32[]{:S(2)}) async-start(), calls=%async_computation.25 | async-start | bytes 417792
  1037.0 1367.0 %all-reduce.10.cloned.1.call-start = ((), (), s32[]{:S(2)}) async-start(), calls=%async_computation.26 | async-start | bytes 7667712 | tf_op jit(solution)/shard_map/psum | solution.py:239
  2310.7 67.1 %copy-start.34 = (bf16[96]{0:T(256)(128)(2,1)S(1)}, bf16[96]{0:T(256)(128)(2,1)}, u32[]{:S(2)}) copy-start(bf16[96]{0:T(256)(128)(2,1)} %dynamic-slice.5) | copy-start | bytes 580
  (28 other events, 108.1 us)
Sparse Core Ops, SparseCore 0:
  10.9 83.8 all-gather.11
  97.6 78.7 all-gather.13
  179.2 78.3 all-gather.9
  260.2 78.3 all-gather.15
  341.3 78.3 all-gather.17
  422.3 150.0 all-gather.21
  575.2 149.5 all-gather.19
  727.6 149.5 all-gather.23
  918.3 136.5 reduce-scatter.19
  1059.9 137.4 reduce-scatter.17
  1202.6 138.0 reduce-scatter.15
  1345.8 137.8 reduce-scatter.13
  1488.8 137.8 reduce-scatter.11
  1632.2 201.6 reduce-scatter.25
  1839.5 202.1 reduce-scatter.23
  2047.2 202.1 reduce-scatter.21
  2254.5 122.4 reduce-scatter.27
  2379.7 24.2 all-reduce.9
where the time goes:
time: 2430 us; the launch traced here: 2420 us
  waiting for transfers between devices  1940 us (80%)
  matrix products  243 us (10%)
  blocking collectives  166 us (7%)
  other arithmetic  30.7 us (1%)
    reduce_scatter x1, waiting for transfers between devices, local(): lax.psum_scatter(grad_up_w.astype(jnp.bfloat16), 'shard', scatter_dimensi...  208 us
    reduce_scatter x1, waiting for transfers between devices, local(): lax.psum_scatter(grad_gate_w.astype(jnp.bfloat16), 'shard', scatter_dimen...  208 us
    reduce_scatter x1, waiting for transfers between devices, local(): lax.psum_scatter(grad_down.astype(jnp.bfloat16), 'shard', scatter_dimensi...  207 us
    all_gather x1, waiting for transfers between devices, local(): up_part = lax.all_gather(w_up, 'shard', axis=0, tiled=True)  146 us
    reduce_scatter x1, waiting for transfers between devices, local(): lax.psum_scatter(grad_value_w.astype(jnp.bfloat16), 'shard', scatter_dime...  143 us
    reduce_scatter x1, waiting for transfers between devices, local(): lax.psum_scatter(grad_query_w.astype(jnp.bfloat16), 'shard', scatter_dime...  143 us
    reduce_scatter x1, waiting for transfers between devices, local(): lax.psum_scatter(grad_key_w.astype(jnp.bfloat16), 'shard', scatter_dimens...  143 us
    all_gather x1, waiting for transfers between devices, local(): gate_part = lax.all_gather(w_gate, 'shard', axis=0, tiled=True)  142 us
  transfers between devices with their start and end apart: 18, of which 16 were waited for; matrix products, arithmetic and copies ran while one was open for 10% of the time, Pallas kernels for 0%

commit v1 on v0

--- a/solution.py
+++ b/solution.py
@@ -9,6 +9,14 @@
 NC = 4
 EPS = 1e-06
 NEGATIVE = -1e30
+
+
+def _put_numbers(inner_x, m, peer_axis):
+    return jnp.split(
+        lax.all_gather(jnp.concatenate([inner_x, m], axis=1), peer_axis, tiled=True, axis=0),
+        [inner_x.shape[1]],
+        axis=1,
+    )
 
 
 def chain_mask(prompt_ids, offsets):
@@ -88,8 +96,7 @@
     gain_part = lax.all_gather(attn_gain, "shard", axis=0, tiled=True)
     query_part = lax.all_gather(w_query, "shard", axis=0, tiled=True)
     key_part = lax.all_gather(w_key, "shard", axis=0, tiled=True)
-    value_part = lax.all_gather(w_value, "shard", axis=0, tiled=True)
-    outgate_part = lax.all_gather(w_outgate, "shard", axis=0, tiled=True)
+    value_part, outgate_part = _put_numbers(w_value, w_outgate, "shard")
     forget_part = lax.all_gather(w_forget, "shard", axis=0, tiled=True)
     normed_part = (scaled1 * gain_part.astype(jnp.float32)).astype(jnp.bfloat16)
     gain_one = gain_part

time: 2430 us -> 2590 us (1.066)
  waiting for transfers between devices: 1940 us -> 2100 us
    reduce_scatter x1, waiting for transfers between devices: 0.01 us -> 143 us  [local(): lax.psum_scatter(grad_output_w.astype(jnp.bfloat16), 'shard', scatter_dim...]
    reduce_scatter x1, waiting for transfers between devices: 143 us -> 7.14 us  [local(): lax.psum_scatter(grad_query_w.astype(jnp.bfloat16), 'shard', scatter_dime...]
    all_gather x0 -> x1, waiting for transfers between devices: none -> 99.9 us  [_put_numbers(): lax.all_gather(jnp.concatenate([inner_x, m], axis=1), peer_axis, tiled=Tr...]
    reduce_scatter x1, waiting for transfers between devices: 110 us -> 143 us  [local(): lax.psum_scatter(grad_outgate_w.astype(jnp.bfloat16), 'shard', scatter_di...]
    all_gather x1, waiting for transfers between devices: 46.6 us -> 74.1 us  [local(): outgate_part = lax.all_gather(w_outgate, 'shard', axis=0, tiled=True)]
    unnamed x19 -> x20, waiting for transfers between devices: 62.1 us -> 66.4 us
  transfers between devices with their start and end apart: 18 -> 19, of which waited for: 16 -> 18; matrix products, arithmetic and copies ran while one was open for 10% -> 8% of each run, Pallas kernels for 0% -> 0%
where the time goes in v1:
time: 2590 us
  waiting for transfers between devices  2100 us (81%)
  matrix products  246 us (9%)
  blocking collectives  165 us (6%)
  other arithmetic  32 us (1%)
    reduce_scatter x1, waiting for transfers between devices, local(): lax.psum_scatter(grad_down.astype(jnp.bfloat16), 'shard', scatter_dimensi...  208 us
    reduce_scatter x1, waiting for transfers between devices, local(): lax.psum_scatter(grad_up_w.astype(jnp.bfloat16), 'shard', scatter_dimensi...  208 us
    reduce_scatter x1, waiting for transfers between devices, local(): lax.psum_scatter(grad_gate_w.astype(jnp.bfloat16), 'shard', scatter_dimen...  207 us
    all_gather x1, waiting for transfers between devices, local(): gate_part = lax.all_gather(w_gate, 'shard', axis=0, tiled=True)  146 us
    reduce_scatter x1, waiting for transfers between devices, local(): lax.psum_scatter(grad_outgate_w.astype(jnp.bfloat16), 'shard', scatter_di...  143 us
    reduce_scatter x1, waiting for transfers between devices, local(): lax.psum_scatter(grad_key_w.astype(jnp.bfloat16), 'shard', scatter_dimens...  143 us
    reduce_scatter x1, waiting for transfers between devices, local(): lax.psum_scatter(grad_value_w.astype(jnp.bfloat16), 'shard', scatter_dime...  143 us
    reduce_scatter x1, waiting for transfers between devices, local(): lax.psum_scatter(grad_output_w.astype(jnp.bfloat16), 'shard', scatter_dim...  143 us
  transfers between devices with their start and end apart: 19, of which 18 were waited for; matrix products, arithmetic and copies ran while one was open for 8% of the time, Pallas kernels for 0%

profile of v1, /device:TPU:0, one launch (start us, length us, event | category | flops | bytes accessed | tf_op | source)
XLA Modules:
  0.0 2585.5 jit_solution(6025729523362079208)
XLA Ops:
  15.1 45.3 %all-reduce.5 = (bf16[1536]{0:T(1024)(128)(2,1)S(1)}, bf16[1536]{0:T(1024)(128)(2,1)S(1)}) all-reduce(bf16[1536]{0:T(1024)(128)(2,1)S(1)} %dynamic-update-slice, bf16[1536]{0:T(1024)(128)(2,1)S(1)} %dynamic-update-slice.1), channel_id=1, replica_groups=mesh['rep'=2,'shard'=16] {'shard'}, use_global_device_ids=true, to_apply=%add | all-reduce | flops 3072 | bytes 12288
  60.5 37.2 %all-gather = bf16[16,96,24]{1,2,0:T(8,128)(2,1)S(1)} all-gather(bf16[1,96,24]{1,2,0:T(8,128)(2,1)S(1)} %bitcast.93), channel_id=1, replica_groups=mesh['rep'=2,'shard'=16] {'shard'}, dimensions={0}, use_global_device_ids=true | all-gather | bytes 78336 | tf_op jit(solution)/shard_map/all_gather | solution.py:100
  105.7 70.7 %all-gather.15.cloned.1.call-done = bf16[1536,1536]{1,0:T(8,128)(2,1)} async-done(((bf16[96,1536]{1,0:T(8,128)(2,1)}), bf16[1536,1536]{1,0:T(8,128)(2,1)}) %all-gather.15.cloned.1.call-update) | async-done | bytes 4718608 | tf_op jit(solution)/shard_map/all_gather | solution.py:98
  200.3 99.9 %all-gather.11.cloned.1.call-done = bf16[1536,3072]{1,0:T(8,128)(2,1)} async-done(((bf16[96,3072]{1,0:T(8,128)(2,1)}), bf16[1536,3072]{1,0:T(8,128)(2,1)}) %all-gather.11.cloned.1.call-update) | async-done | bytes 9437200 | tf_op jit(solution)/shard_map/all_gather | solution.py:16
  305.4 9.8 fusion.10
  324.7 56.2 %all-gather.17.cloned.1.call-done = bf16[1536,1536]{1,0:T(8,128)(2,1)} async-done(((bf16[96,1536]{1,0:T(8,128)(2,1)}), bf16[1536,1536]{1,0:T(8,128)(2,1)}) %all-gather.17.cloned.1.call-update) | async-done | bytes 4718608 | tf_op jit(solution)/shard_map/all_gather | solution.py:125
  387.6 146.0 %all-gather.19.cloned.1.call-done = bf16[1536,4096]{1,0:T(8,128)(2,1)} async-done(((bf16[96,4096]{1,0:T(8,128)(2,1)}), bf16[1536,4096]{1,0:T(8,128)(2,1)}) %all-gather.19.cloned.1.call-update) | async-done | bytes 12582928 | tf_op jit(solution)/shard_map/all_gather | solution.py:129
  533.6 10.0 fusion.103
  543.6 142.3 %all-gather.21.cloned.1.call-done = bf16[1536,4096]{1,0:T(8,128)(2,1)} async-done(((bf16[96,4096]{1,0:T(8,128)(2,1)}), bf16[1536,4096]{1,0:T(8,128)(2,1)}) %all-gather.21.cloned.1.call-update) | async-done | bytes 12582928 | tf_op jit(solution)/shard_map/all_gather | solution.py:130
  685.9 10.0 fusion.104
  695.8 142.4 %all-gather.23.cloned.1.call-done = bf16[4096,1536]{1,0:T(8,128)(2,1)} async-done(((bf16[256,1536]{1,0:T(8,128)(2,1)}), bf16[4096,1536]{1,0:T(8,128)(2,1)}) %all-gather.23.cloned.1.call-update) | async-done | bytes 12582928 | tf_op jit(solution)/shard_map/all_gather | solution.py:137
  838.3 15.2 multiply_convert_fusion.1
  853.5 9.7 fusion.105
  863.3 9.3 multiply_reduce_fusion.1
  881.7 22.4 fusion.99
  955.6 11.6 convolution_convert_fusion.2
  967.3 11.5 convolution_convert_fusion.1
  978.9 11.3 convolution_convert_fusion
  1008.2 39.3 %psum.90 = f32[24]{0:T(128)} all-reduce(f32[24]{0:T(128)S(1)} %get-tuple-element.53), channel_id=1, replica_groups=mesh['rep'=2,'shard'=16] {'rep','shard'}, use_global_device_ids=true, to_apply=%region_25.26 | all-reduce | flops 24 | bytes 192 | tf_op jit(solution)/shard_map/psum | solution.py:195
  1054.7 143.3 %reduce-scatter.14.cloned.1.call-done = bf16[96,1536]{1,0:T(8,128)(2,1)} async-done(((bf16[1536,1536]{1,0:T(8,128)(2,1)}), bf16[96,1536]{1,0:T(8,128)(2,1)}) %reduce-scatter.14.cloned.1.call-update) | async-done | bytes 294928 | tf_op jit(solution)/shard_map/reduce_scatter | solution.py:228
  1197.9 143.0 %reduce-scatter.16.cloned.1.call-done = bf16[96,1536]{1,0:T(8,128)(2,1)} async-done(((bf16[1536,1536]{1,0:T(8,128)(2,1)}), bf16[96,1536]{1,0:T(8,128)(2,1)}) %reduce-scatter.16.cloned.1.call-update) | async-done | bytes 294928 | tf_op jit(solution)/shard_map/reduce_scatter | solution.py:231
  1341.0 143.4 %reduce-scatter.18.cloned.1.call-done = bf16[96,1536]{1,0:T(8,128)(2,1)} async-done(((bf16[1536,1536]{1,0:T(8,128)(2,1)}), bf16[96,1536]{1,0:T(8,128)(2,1)}) %reduce-scatter.18.cloned.1.call-update) | async-done | bytes 294928 | tf_op jit(solution)/shard_map/reduce_scatter | solution.py:234
  1484.4 142.9 %reduce-scatter.20.cloned.1.call-done = bf16[96,1536]{1,0:T(8,128)(2,1)} async-done(((bf16[1536,1536]{1,0:T(8,128)(2,1)}), bf16[96,1536]{1,0:T(8,128)(2,1)}) %reduce-scatter.20.cloned.1.call-update) | async-done | bytes 294928 | tf_op jit(solution)/shard_map/reduce_scatter | solution.py:240
  1627.3 207.4 %reduce-scatter.22.cloned.1.call-done = bf16[96,4096]{1,0:T(8,128)(2,1)} async-done(((bf16[1536,4096]{1,0:T(8,128)(2,1)}), bf16[96,4096]{1,0:T(8,128)(2,1)}) %reduce-scatter.22.cloned.1.call-update) | async-done | bytes 786448 | tf_op jit(solution)/shard_map/reduce_scatter | solution.py:157
  1834.7 207.7 %reduce-scatter.24.cloned.1.call-done = bf16[96,4096]{1,0:T(8,128)(2,1)} async-done(((bf16[1536,4096]{1,0:T(8,128)(2,1)}), bf16[96,4096]{1,0:T(8,128)(2,1)}) %reduce-scatter.24.cloned.1.call-update) | async-done | bytes 786448 | tf_op jit(solution)/shard_map/reduce_scatter | solution.py:160
  2042.4 207.9 %reduce-scatter.26.cloned.1.call-done = bf16[256,1536]{1,0:T(8,128)(2,1)} async-done(((bf16[4096,1536]{1,0:T(8,128)(2,1)}), bf16[256,1536]{1,0:T(8,128)(2,1)}) %reduce-scatter.26.cloned.1.call-update) | async-done | bytes 786448 | tf_op jit(solution)/shard_map/reduce_scatter | solution.py:163
  2250.3 81.8 %all-gather.25.cloned.1.call-done = bf16[1536,1536]{1,0:T(8,128)(2,1)} async-done(((bf16[96,1536]{1,0:T(8,128)(2,1)}), bf16[1536,1536]{1,0:T(8,128)(2,1)}) %all-gather.25.cloned.1.call-update) | async-done | bytes 4718608 | tf_op jit(solution)/shard_map/all_gather | solution.py:202
  2339.0 74.1 %all-gather.27.cloned.1.call-done = bf16[1536,1536]{1,0:T(8,128)(2,1)} async-done(((bf16[96,1536]{1,0:T(8,128)(2,1)}), bf16[1536,1536]{1,0:T(8,128)(2,1)}) %all-gather.27.cloned.1.call-update) | async-done | bytes 4718608 | tf_op jit(solution)/shard_map/all_gather | solution.py:203
  2421.5 41.0 %all-reduce.4 = (bf16[1536]{0:T(1024)(128)(2,1)}, bf16[1536]{0:T(1024)(128)(2,1)}) all-reduce(bf16[1536]{0:T(1024)(128)(2,1)S(1)} %get-tuple-element.18, bf16[1536]{0:T(1024)(128)(2,1)} %get-tuple-element.16), channel_id=2, replica_groups=mesh['rep'=2,'shard'=16] {'shard'}, use_global_device_ids=true, to_apply=%region_12.13.clone | all-reduce | flops 3072 | bytes 12288
  2469.1 9.3 fusion.29
  2478.4 61.5 %reduce-scatter.28.cloned.1.call-done = bf16[96,24]{1,0:T(8,128)(2,1)} async-done(((bf16[1536,24]{1,0:T(8,128)(2,1)}), bf16[96,24]{1,0:T(8,128)(2,1)}) %reduce-scatter.28.cloned.1.call-update) | async-done | bytes 4624
  2544.9 22.2 all-reduce.10.cloned.1.call-done
  (200 shorter events, 183.2 us)
Async XLA Ops:
  7.2 93.2 %all-gather.13.cloned.1.call-start = ((), (), s32[]{:S(2)}) async-start(), calls=%async_computation.10 | async-start | bytes 5013504 | tf_op jit(solution)/shard_map/all_gather | solution.py:97
  7.9 52.5 %copy-start.31 = (bf16[96,24]{0,1:T(8,128)(2,1)S(1)}, bf16[96,24]{0,1:T(8,128)(2,1)}, u32[]{:S(2)}) copy-start(bf16[96,24]{0,1:T(8,128)(2,1)} %param.24) | copy-start | bytes 13828
  8.0 168.4 %all-gather.15.cloned.1.call-start = ((), (), s32[]{:S(2)}) async-start(), calls=%async_computation.11 | async-start | bytes 5013504 | tf_op jit(solution)/shard_map/all_gather | solution.py:98
  8.7 89.2 %copy-start.38 = (bf16[24]{0:T(256)(128)(2,1)S(1)}, bf16[24]{0:T(256)(128)(2,1)}, u32[]{:S(2)}) copy-start(bf16[24]{0:T(256)(128)(2,1)} %param.25) | copy-start | bytes 148
  8.7 89.3 %copy-start.33 = (s32[1,4]{1,0:T(1,128)S(1)}, s32[1,4]{1,0:T(1,128)}, u32[]{:S(2)}) copy-start(s32[1,4]{1,0:T(1,128)} %param.17) | copy-start | bytes 52
  8.7 89.3 %copy-start.34 = (s32[1,4]{1,0:T(1,128)S(1)}, s32[1,4]{1,0:T(1,128)}, u32[]{:S(2)}) copy-start(s32[1,4]{1,0:T(1,128)} %param.18) | copy-start | bytes 52
  8.7 89.4 %copy-start = (bf16[384,1536]{1,0:T(8,128)(2,1)S(1)}, bf16[384,1536]{1,0:T(8,128)(2,1)}, u32[]{:S(2)}) copy-start(bf16[384,1536]{1,0:T(8,128)(2,1)} %param.16) | copy-start | bytes 3538948
  8.7 291.5 %all-gather.11.cloned.1.call-start = ((), (), s32[]{:S(2)}) async-start(), calls=%async_computation.9 | async-start | bytes 10027008 | tf_op jit(solution)/shard_map/all_gather | solution.py:16
  10.8 370.1 %all-gather.17.cloned.1.call-start = ((), (), s32[]{:S(2)}) async-start(), calls=%async_computation.12 | async-start | bytes 5013504 | tf_op jit(solution)/shard_map/all_gather | solution.py:125
  11.4 522.2 %all-gather.19.cloned.1.call-start = ((), (), s32[]{:S(2)}) async-start(), calls=%async_computation.13 | async-start | bytes 13369344 | tf_op jit(solution)/shard_map/all_gather | solution.py:129
  12.0 673.9 %all-gather.21.cloned.1.call-start = ((), (), s32[]{:S(2)}) async-start(), calls=%async_computation.14 | async-start | bytes 13369344 | tf_op jit(solution)/shard_map/all_gather | solution.py:130
  12.6 825.7 %all-gather.23.cloned.1.call-start = ((), (), s32[]{:S(2)}) async-start(), calls=%async_computation.15 | async-start | bytes 13369344 | tf_op jit(solution)/shard_map/all_gather | solution.py:137
  13.3 1041.3 %reduce-scatter.12.cloned.1.call-start = ((), (), s32[]{:S(2)}) async-start(), calls=%async_computation.18 | async-start | bytes 5013504 | tf_op jit(solution)/shard_map/reduce_scatter | solution.py:225
  105.7 77.8 %copy-start.5 = (bf16[384,1536]{0,1:T(8,128)(2,1)}, bf16[384,1536]{0,1:T(8,128)(2,1)S(1)}, u32[]{:S(2)}) copy-start(bf16[384,1536]{0,1:T(8,128)(2,1)S(1)} %copy.67) | copy-start | bytes 3538948
  191.7 108.6 %copy-start.27 = (f32[384]{0:T(512)S(1)}, f32[384]{0:T(512)}, u32[]{:S(2)}) copy-start(f32[384]{0:T(512)} %copy-done.26) | copy-start | bytes 4612
  385.7 477.6 %copy-start.3 = (f32[384,1536]{1,0:T(8,128)}, f32[384,1536]{1,0:T(8,128)S(1)}, u32[]{:S(2)}) copy-start(f32[384,1536]{1,0:T(8,128)S(1)} %get-tuple-element.49) | copy-start | bytes 7077892
  853.5 9.8 copy-start.30
  853.5 9.8 copy-start.40
  853.5 21.6 slice-start
  863.3 11.8 slice-start.1
  916.7 281.3 %reduce-scatter.14.cloned.1.call-start = ((), (), s32[]{:S(2)}) async-start(), calls=%async_computation.19 | async-start | bytes 5013504 | tf_op jit(solution)/shard_map/reduce_scatter | solution.py:228
  930.3 410.7 %reduce-scatter.16.cloned.1.call-start = ((), (), s32[]{:S(2)}) async-start(), calls=%async_computation.20 | async-start | bytes 5013504 | tf_op jit(solution)/shard_map/reduce_scatter | solution.py:231
  944.0 540.4 %reduce-scatter.18.cloned.1.call-start = ((), (), s32[]{:S(2)}) async-start(), calls=%async_computation.21 | async-start | bytes 5013504 | tf_op jit(solution)/shard_map/reduce_scatter | solution.py:234
  949.9 677.5 %reduce-scatter.20.cloned.1.call-start = ((), (), s32[]{:S(2)}) async-start(), calls=%async_computation.22 | async-start | bytes 5013504 | tf_op jit(solution)/shard_map/reduce_scatter | solution.py:240
  955.6 879.1 %reduce-scatter.22.cloned.1.call-start = ((), (), s32[]{:S(2)}) async-start(), calls=%async_computation.23 | async-start | bytes 13369344 | tf_op jit(solution)/shard_map/reduce_scatter | solution.py:157
  967.3 1075.1 %reduce-scatter.24.cloned.1.call-start = ((), (), s32[]{:S(2)}) async-start(), calls=%async_computation.24 | async-start | bytes 13369344 | tf_op jit(solution)/shard_map/reduce_scatter | solution.py:160
  978.8 1271.4 %reduce-scatter.26.cloned.1.call-start = ((), (), s32[]{:S(2)}) async-start(), calls=%async_computation.25 | async-start | bytes 13369344 | tf_op jit(solution)/shard_map/reduce_scatter | solution.py:163
  990.3 1341.9 %all-gather.25.cloned.1.call-start = ((), (), s32[]{:S(2)}) async-start(), calls=%async_computation.16 | async-start | bytes 5013504 | tf_op jit(solution)/shard_map/all_gather | solution.py:202
  990.8 1422.3 %all-gather.27.cloned.1.call-start = ((), (), s32[]{:S(2)}) async-start(), calls=%async_computation.17 | async-start | bytes 5013504 | tf_op jit(solution)/shard_map/all_gather | solution.py:203
  991.4 1548.5 %reduce-scatter.28.cloned.1.call-start = ((), (), s32[]{:S(2)}) async-start(), calls=%async_computation.26 | async-start | bytes 417792
  997.1 1570.0 %all-reduce.10.cloned.1.call-start = ((), (), s32[]{:S(2)}) async-start(), calls=%async_computation.27 | async-start | bytes 7667712 | tf_op jit(solution)/shard_map/psum | solution.py:246
  2469.1 71.6 %copy-start.35 = (bf16[96]{0:T(256)(128)(2,1)S(1)}, bf16[96]{0:T(256)(128)(2,1)}, u32[]{:S(2)}) copy-start(bf16[96]{0:T(256)(128)(2,1)} %dynamic-slice.5) | copy-start | bytes 580
  (31 other events, 135.9 us)
Sparse Core Ops, SparseCore 0:
  10.8 83.7 all-gather.12
  97.4 78.9 all-gather.14
  179.8 120.3 all-gather.10
  302.9 77.9 all-gather.16
  383.5 150.0 all-gather.18
  536.2 149.5 all-gather.20
  688.6 149.5 all-gather.22
  916.8 137.8 reduce-scatter.11
  1059.8 138.0 reduce-scatter.13
  1203.0 137.9 reduce-scatter.15
  1346.1 138.2 reduce-scatter.17
  1489.4 137.8 reduce-scatter.19
  1633.0 201.6 reduce-scatter.21
  1840.2 202.1 reduce-scatter.23
  2047.9 202.3 reduce-scatter.25
  2252.9 79.1 all-gather.24
  2334.8 78.3 all-gather.26
  2418.3 121.6 reduce-scatter.27
  2542.8 24.2 all-reduce.9
